TPU v7x, 256 devices: a whole 4x4x8 slice. The times are simulated.
256 devices in a mesh: fsdp: 2 (over y_hi), dp: 32 (over x, z), owner: 4 (over y_lo, core).
Axes of the slice: x: 4, y: 4 (y_hi: 2, y_lo: 2; y = y_hi * 2 + y_lo), z: 8, core: 2. Of those that a mesh axis runs over, the one named last changes fastest.
Arguments:
- hidden: bfloat16 [256, 256, 4096], P(('fsdp', 'dp', 'owner')), may hold values from -6 to 6
- norm_gain: float32 [4096], replicated, may hold values from 0.1 to 1.9
- query_weight: bfloat16 [4096, 2048], P(('fsdp', 'dp')), may hold values from -0.09375 to 0.09375
- key_value_weight: bfloat16 [4096, 1024], P(('fsdp', 'dp')), may hold values from -0.09375 to 0.09375
- lengths: int32 [256], P(('fsdp', 'dp', 'owner')), may hold values from 128 to 256, as said below
- cotangent: bfloat16 [256, 256, 2048], P(('fsdp', 'dp', 'owner')), may hold values from -6 to 6
- cartridge: float32 [512, 1024], P('owner'), may hold values from -48 to 48
- adam_first_moment: float32 [512, 1024], P('owner'), may hold values from -6 to 6
- adam_second_moment: float32 [512, 1024], P('owner'), may hold values from 0.01 to 1
Outputs:
- attention_out: bfloat16 [256, 256, 2048], P(('fsdp', 'dp', 'owner'))
- new_cartridge: float32 [512, 1024], P('owner')
- new_first: float32 [512, 1024], P('owner')
- new_second: float32 [512, 1024], P('owner')
Inputs may be any that keep to these rules, and one draw needn't show every extreme that they name: `lengths`: each conversation's live tokens are its first rows; the rows after them are padding; some conversation is full.
All inputs are finite; a program needn't handle non-finite values.
Results may differ from a plain program's by a relative error of at most 0.008.
The roundings to bfloat16 on the way count: a program that leaves them out, or rounds other values in their place, can miss the bound.
Values may be sent and summed in bfloat16 or wider, within the bound.
No kernel may reach another device: no remote copies, remote signals or barrier semaphores. Data moves between devices by JAX's collectives and lax.ppermute only.
A program may use at most 128 MiB of HBM per device.

v0:
```python
import jax
import jax.numpy as jnp
from jax import lax
from jax.sharding import PartitionSpec as P

HEAD_SIZE = 128
QUERY_HEADS = 16
KEY_VALUE_HEADS = 4
STEP = 50


def rotary_heads(values, offset):
    sequence_rows = values.shape[0]
    half_size = values.shape[2] // 2
    exponent = jnp.arange(half_size, dtype=jnp.float32) * (2.0 / values.shape[2])
    inverse = jnp.power(jnp.float32(500000.0), -exponent)
    position = (offset + jnp.arange(sequence_rows)).astype(jnp.float32)
    angles = position[:, None] * inverse[None, :]
    cosine = jnp.cos(angles)[:, None, :]
    sine = jnp.sin(angles)[:, None, :]
    first_half = values[..., :half_size]
    second_half = values[..., half_size:]
    return jnp.concatenate(
        [first_half * cosine - second_half * sine, second_half * cosine + first_half * sine],
        axis=-1,
    )


def adam_update(current, moment_one, moment_two, prefix_gradient):
    one_new = 0.9 * moment_one + 0.1 * prefix_gradient
    two_new = 0.999 * moment_two + 0.001 * prefix_gradient * prefix_gradient
    one_fix = 1.0 - 0.9**STEP
    two_fix = 1.0 - 0.999**STEP
    updated = current - 0.02 * (one_new / one_fix) / (jnp.sqrt(two_new / two_fix) + 1e-08)
    return (updated, one_new, two_new)


def add_rows(pieces, features):
    return (
        jnp.dot(features, pieces[0], preferred_element_type=jnp.float32),
        jnp.dot(features, pieces[1], preferred_element_type=jnp.float32),
    )


def on_device(
    hidden,
    norm_gain,
    query_weight,
    key_value_weight,
    lengths,
    cotangent,
    cartridge,
    adam_first_moment,
    adam_second_moment,
):
    sequence_rows = hidden.shape[1]
    query_group_size = QUERY_HEADS // KEY_VALUE_HEADS
    score_scale = HEAD_SIZE ** (-0.5)
    states = hidden[0].astype(jnp.float32)
    normed = (
        states * lax.rsqrt(jnp.mean(states * states, axis=1, keepdims=True) + 1e-05) * norm_gain
    ).astype(jnp.bfloat16)
    proj_query, project_key_value = add_rows(
        (
            lax.all_gather(query_weight, ("fsdp", "dp"), axis=0, tiled=True),
            lax.all_gather(key_value_weight, ("fsdp", "dp"), axis=0, tiled=True),
        ),
        normed,
    )
    shard_rows = cartridge.shape[0]
    prefix_length = shard_rows * lax.axis_size("owner")
    query_rows = rotary_heads(
        proj_query.reshape(sequence_rows, QUERY_HEADS, HEAD_SIZE), prefix_length
    ).astype(jnp.bfloat16)
    sequence_keys = rotary_heads(
        project_key_value[:, : KEY_VALUE_HEADS * HEAD_SIZE].reshape(
            sequence_rows, KEY_VALUE_HEADS, HEAD_SIZE
        ),
        prefix_length,
    ).astype(jnp.bfloat16)
    sequence_values = (
        project_key_value[:, KEY_VALUE_HEADS * HEAD_SIZE :]
        .reshape(sequence_rows, KEY_VALUE_HEADS, HEAD_SIZE)
        .astype(jnp.bfloat16)
    )
    gathered_rows = lax.all_gather(cartridge.astype(jnp.bfloat16), "owner", axis=0, tiled=True)
    cartridge_keys = gathered_rows[:, : KEY_VALUE_HEADS * HEAD_SIZE].reshape(
        prefix_length, KEY_VALUE_HEADS, HEAD_SIZE
    )
    cartridge_values = gathered_rows[:, KEY_VALUE_HEADS * HEAD_SIZE :].reshape(
        prefix_length, KEY_VALUE_HEADS, HEAD_SIZE
    )
    grouped_heads = query_rows.reshape(sequence_rows, KEY_VALUE_HEADS, query_group_size, HEAD_SIZE)
    pre_scores = (
        jnp.einsum(
            "shgd,phd->hgsp", grouped_heads, cartridge_keys, preferred_element_type=jnp.float32
        )
        * score_scale
    )
    own_scores = (
        jnp.einsum(
            "shgd,thd->hgst", grouped_heads, sequence_keys, preferred_element_type=jnp.float32
        )
        * score_scale
    )
    causal = jnp.arange(sequence_rows)[:, None] >= jnp.arange(sequence_rows)[None, :]
    own_scores = jnp.where(causal, own_scores, -jnp.inf)
    highest = jnp.maximum(
        jnp.max(pre_scores, axis=-1, keepdims=True), jnp.max(own_scores, axis=-1, keepdims=True)
    )
    pre_exp = jnp.exp(pre_scores - highest)
    own_exp = jnp.exp(own_scores - highest)
    denominator = jnp.sum(pre_exp, axis=-1, keepdims=True) + jnp.sum(
        own_exp, axis=-1, keepdims=True
    )
    pre_probs = pre_exp / denominator
    pre_low = pre_probs.astype(jnp.bfloat16)
    own_low = (own_exp / denominator).astype(jnp.bfloat16)
    attended = jnp.einsum(
        "hgsp,phd->shgd", pre_low, cartridge_values, preferred_element_type=jnp.float32
    )
    attended = attended + jnp.einsum(
        "hgst,thd->shgd", own_low, sequence_values, preferred_element_type=jnp.float32
    )
    active_rows = (jnp.arange(sequence_rows) < lengths[0])[:, None, None, None]
    attention_out = jnp.where(active_rows, attended, 0.0).astype(jnp.bfloat16)
    upstream_gradient = jnp.where(
        active_rows,
        cotangent[0].reshape(sequence_rows, KEY_VALUE_HEADS, query_group_size, HEAD_SIZE),
        0.0,
    )
    delta = jnp.einsum(
        "shgd,shgd->hgs", upstream_gradient, attention_out, preferred_element_type=jnp.float32
    )
    dprob = jnp.einsum(
        "shgd,phd->hgsp", upstream_gradient, cartridge_values, preferred_element_type=jnp.float32
    )
    dscore = (pre_probs * (dprob - delta[..., None])).astype(jnp.bfloat16)
    gradient_keys = (
        jnp.einsum("hgsp,shgd->phd", dscore, grouped_heads, preferred_element_type=jnp.float32)
        * score_scale
    )
    gradient_values = jnp.einsum(
        "hgsp,shgd->phd", pre_low, upstream_gradient, preferred_element_type=jnp.float32
    )
    prefix_gradient = jnp.concatenate(
        [
            gradient_keys.reshape(prefix_length, KEY_VALUE_HEADS * HEAD_SIZE),
            gradient_values.reshape(prefix_length, KEY_VALUE_HEADS * HEAD_SIZE),
        ],
        axis=1,
    )
    summed = lax.psum(prefix_gradient, ("fsdp", "dp", "owner"))
    owned_sum = lax.dynamic_slice_in_dim(
        summed, lax.axis_index("owner") * shard_rows, shard_rows, 0
    )
    new_cartridge, new_first, new_second = adam_update(
        cartridge, adam_first_moment, adam_second_moment, owned_sum
    )
    return (
        attention_out.reshape(1, sequence_rows, QUERY_HEADS * HEAD_SIZE),
        new_cartridge,
        new_first,
        new_second,
    )


def solution(mesh):
    placed = (
        P(("fsdp", "dp", "owner"), None, None),
        P(),
        P(("fsdp", "dp"), None),
        P(("fsdp", "dp"), None),
        P(("fsdp", "dp", "owner")),
        P(("fsdp", "dp", "owner"), None, None),
        P("owner", None),
        P("owner", None),
        P("owner", None),
    )
    return jax.shard_map(
        on_device,
        mesh=mesh,
        in_specs=placed,
        out_specs=(
            P(("fsdp", "dp", "owner"), None, None),
            P("owner", None),
            P("owner", None),
            P("owner", None),
        ),
        check_vma=False,
    )
```

profile of v0, /device:TPU:2, one launch (start us, length us, event | category | flops | bytes accessed | tf_op | source)
XLA Modules:
  0.0 717.0 jit_solution(16635561501502723550)
XLA Ops:
  7.2 2.0 copy.31
  12.0 2.3 copy.39
  14.8 21.3 %all-gather.6.cloned.1.call-done = bf16[512,1024]{0,1:T(8,128)(2,1)} async-done(((bf16[128,1024]{0,1:T(8,128)(2,1)}), bf16[512,1024]{0,1:T(8,128)(2,1)}) %all-gather.6.cloned.1.call-update) | async-done | bytes 1048592 | tf_op jit(solution)/shard_map/all_gather | solution.py:86
  36.1 2.1 fusion.62
  38.2 149.8 %all-gather.8.cloned.1.call-done = bf16[4096,1024]{1,0:T(8,128)(2,1)} async-done(((bf16[64,1024]{1,0:T(8,128)(2,1)}), bf16[4096,1024]{1,0:T(8,128)(2,1)}) %all-gather.8.cloned.1.call-update) | async-done | bytes 8388624 | tf_op jit(solution)/shard_map/all_gather | solution.py:66
  188.0 5.8 fusion.22
  195.2 0.8 subtract_convert_fusion.1
  196.1 191.2 %all-gather.4.cloned.1.call-done = bf16[4096,2048]{1,0:T(8,128)(2,1)} async-done(((bf16[64,2048]{1,0:T(8,128)(2,1)}), bf16[4096,2048]{1,0:T(8,128)(2,1)}) %all-gather.4.cloned.1.call-update) | async-done | bytes 16777232 | tf_op jit(solution)/shard_map/all_gather | solution.py:65
  387.3 21.5 %copy.28 = bf16[2048,4096]{1,0:T(8,128)(2,1)} copy(bf16[2048,4096]{0,1:T(8,128)(2,1)} %bitcast.119) | data formatting | bytes 33554432 | tf_op jit(solution)/shard_map/dot_general | solution.py:40
  408.9 8.3 %fusion.20 = f32[256,16,128]{0,2,1:T(8,128)S(1)} fusion(bf16[16,128,4096]{2,1,0:T(8,128)(2,1)} %bitcast.120, bf16[1,256,4096]{2,1,0:T(8,128)(2,1)S(1)} %copy-done.2, f32[4096]{0:T(1024)S(1)} %copy-done.12, f32[256]{0:T(256)S(1)} %add_rsqrt_fusion), kind=kOutput, calls=%fused_computation.26 | convolution fusion | flops 4299161600 | bytes 20988928 | tf_op jit(solution)/shard_map/dot_general | solution.py:40
  418.5 1.5 bitcast_reduce_fusion
  420.1 1.4 fusion.18
  421.5 0.9 fusion.17
  422.4 2.2 fusion.4
  424.7 1.6 fusion.35
  426.3 3.5 fusion.27
  429.8 4.0 fusion.24
  433.8 8.9 %fusion.41 = f32[4,128,512]{2,1,0:T(8,128)} fusion(f32[4,4,256]{2,1,0:T(4,128)S(1)} %get-tuple-element.29, bf16[512,4,128,1]{0,2,3,1:T(8,128)(2,1)} %bitcast.130, bf16[256,4,4,128]{0,3,2,1:T(8,128)(2,1)S(1)} %bitcast.126, pred[256]{0:T(512)(128)(4,1)S(1)} %iota_compare_fusion.1, bf16[256,4,4,64]{3,0,2,1:T(8,128)(2,1)S(1)} %copy.30, ...), kind=kOutput, calls=%fused_computation.44 | convolution fusion | flops 1089208320 | bytes 12108032 | tf_op jit(solution)/shard_map/hgsp,shgd->phd/dot_general | solution.py:140
  442.7 1.6 copy.42
  444.2 1.6 copy.41
  445.8 1.5 pad_maximum_fusion
  447.3 2.3 copy.43
  449.7 258.4 %all-reduce.2.cloned.1.call-done = f32[512,1024]{1,0:T(8,128)} async-done(((f32[512,1024]{1,0:T(8,128)}), f32[512,1024]{1,0:T(8,128)}) %all-reduce.2.cloned.1.call-update) | async-done | bytes 2097168 | tf_op jit(solution)/shard_map/psum | solution.py:153
  708.0 2.4 divide_subtract_fusion
  (53 shorter events, 5.4 us)
Async XLA Ops:
  7.2 7.1 copy-start.1
  7.2 180.8 %copy-start.12 = (f32[4096]{0:T(1024)S(1)}, f32[4096]{0:T(1024)}, u32[]{:S(2)}) copy-start(f32[4096]{0:T(1024)} %param.10) | copy-start | bytes 49156
  7.2 29.0 %all-gather.6.cloned.1.call-start = ((), (), s32[]{:S(2)}) async-start(), calls=%async_computation.1 | async-start | bytes 1310720 | tf_op jit(solution)/shard_map/all_gather | solution.py:86
  9.3 178.7 %all-gather.8.cloned.1.call-start = ((), (), s32[]{:S(2)}) async-start(), calls=%async_computation.2 | async-start | bytes 8519680 | tf_op jit(solution)/shard_map/all_gather | solution.py:66
  10.0 377.3 %all-gather.4.cloned.1.call-start = ((), (), s32[]{:S(2)}) async-start(), calls=%async_computation | async-start | bytes 17039360 | tf_op jit(solution)/shard_map/all_gather | solution.py:65
  10.8 697.3 %all-reduce.2.cloned.1.call-start = ((), (), s32[]{:S(2)}) async-start(), calls=%async_computation.3 | async-start | bytes 4194304 | tf_op jit(solution)/shard_map/psum | solution.py:153
  11.8 3.0 copy-start.6
  387.3 21.6 %copy-start.2 = (bf16[1,256,4096]{2,1,0:T(8,128)(2,1)S(1)}, bf16[1,256,4096]{2,1,0:T(8,128)(2,1)}, u32[]{:S(2)}) copy-start(bf16[1,256,4096]{2,1,0:T(8,128)(2,1)} %param.9) | copy-start | bytes 6291460
  408.9 8.4 %copy-start.7 = (f32[256,64]{0,1:T(8,128)S(1)}, f32[256,64]{0,1:T(8,128)}, u32[]{:S(2)}) copy-start(f32[256,64]{0,1:T(8,128)} %copy-done.6) | copy-start | bytes 196612
  418.5 1.6 copy-start.5
  420.1 9.7 %copy-start = (f32[4,256,4,512]{3,1,2,0:T(8,128)}, f32[4,256,4,512]{3,1,2,0:T(8,128)S(1)}, u32[]{:S(2)}) copy-start(f32[4,256,4,512]{3,1,2,0:T(8,128)S(1)} %get-tuple-element.26) | copy-start | bytes 25165828
  422.4 2.2 copy-start.11
  424.6 1.6 copy-start.4
  426.3 3.5 copy-start.10
  445.8 262.2 %copy-start.3 = (f32[128,1024]{1,0:T(8,128)S(1)}, f32[128,1024]{1,0:T(8,128)}, u32[]{:S(2)}) copy-start(f32[128,1024]{1,0:T(8,128)} %param.15) | copy-start | bytes 1572868
  445.8 262.2 %copy-start.8 = (f32[128,1024]{1,0:T(8,128)S(1)}, f32[128,1024]{1,0:T(8,128)}, u32[]{:S(2)}) copy-start(f32[128,1024]{1,0:T(8,128)} %param.16) | copy-start | bytes 1572868
  447.3 260.7 %copy-start.9 = (f32[128,1024]{1,0:T(8,128)S(1)}, f32[128,1024]{1,0:T(8,128)}, u32[]{:S(2)}) copy-start(f32[128,1024]{1,0:T(8,128)} %param.17) | copy-start | bytes 1572868
Sparse Core Ops, SparseCore 0:
  10.4 25.7 all-gather.5
  39.8 148.1 all-gather.7
  191.7 195.5 all-gather.3
  447.5 260.5 all-reduce.1
where the time goes:
time: 718 us; the launch traced here: 717 us
  waiting for transfers between devices  622 us (87%)
  local copies, waits for them, and re-layouts  36 us (5%)
  matrix products  35 us (5%)
  between operations  14.7 us (2%)
  other arithmetic  9.01 us (1%)
    psum x1, waiting for transfers between devices, on_device(): summed = lax.psum(prefix_gradient, ('fsdp', 'dp', 'owner'))  258 us
    all_gather x1, waiting for transfers between devices, on_device(): lax.all_gather(query_weight, ('fsdp', 'dp'), axis=0, tiled=True)  191 us
    all_gather x1, waiting for transfers between devices, on_device(): lax.all_gather(key_value_weight, ('fsdp', 'dp'), axis=0, tiled=True)  150 us
    dot_general x1, local copies, waits for them, and re-layouts, add_rows(): jnp.dot(features, pieces[0], preferred_element_type=jnp.float32)  21.5 us
    all_gather x1, waiting for transfers between devices, on_device(): lax.all_gather(cartridge.astype(jnp.bfloat16), 'owner', axis=0, tiled=True)  21.3 us
  transfers between devices with their start and end apart: 4, of which 4 were waited for; matrix products, arithmetic and copies ran while one was open for 2% of the time, Pallas kernels for 0%

commit v1 on v0

--- a/solution.py
+++ b/solution.py
@@ -150,7 +150,7 @@
         ],
         axis=1,
     )
-    summed = lax.psum(prefix_gradient, ("fsdp", "dp", "owner"))
+    summed = lax.psum(lax.psum(prefix_gradient, "fsdp"), ("dp", "owner"))
     owned_sum = lax.dynamic_slice_in_dim(
         summed, lax.axis_index("owner") * shard_rows, shard_rows, 0
     )

time: 718 us -> 1630 us (2.27)
  the two profiles are of different devices: /device:TPU:2 before, /device:TPU:16 now
where the time goes in v1:
time: 1630 us
  waiting for transfers between devices  1540 us (94%)
  matrix products  35.1 us (2%)
  local copies, waits for them, and re-layouts  34.4 us (2%)
    psum x2, waiting for transfers between devices, on_device(): summed = lax.psum(lax.psum(prefix_gradient, 'fsdp'), ('dp', 'owner'))  1180 us
    all_gather x1, waiting for transfers between devices, on_device(): lax.all_gather(query_weight, ('fsdp', 'dp'), axis=0, tiled=True)  191 us
    all_gather x1, waiting for transfers between devices, on_device(): lax.all_gather(key_value_weight, ('fsdp', 'dp'), axis=0, tiled=True)  147 us
  transfers between devices with their start and end apart: 5, of which 5 were waited for; matrix products, arithmetic and copies ran while one was open for 1% of the time, Pallas kernels for 0%

profile of v1, /device:TPU:16, one launch (start us, length us, event | category | flops | bytes accessed | tf_op | source)
XLA Modules:
  0.0 1632.2 jit_solution(17208073496898405009)
XLA Ops:
  7.2 2.0 copy.31
  12.0 2.3 copy.39
  14.8 21.2 %all-gather.6.cloned.1.call-done = bf16[512,1024]{0,1:T(8,128)(2,1)} async-done(((bf16[128,1024]{0,1:T(8,128)(2,1)}), bf16[512,1024]{0,1:T(8,128)(2,1)}) %all-gather.6.cloned.1.call-update) | async-done | bytes 1048592 | tf_op jit(solution)/shard_map/all_gather | solution.py:86
  36.0 2.1 fusion.62
  38.0 147.3 %all-gather.8.cloned.1.call-done = bf16[4096,1024]{1,0:T(8,128)(2,1)} async-done(((bf16[64,1024]{1,0:T(8,128)(2,1)}), bf16[4096,1024]{1,0:T(8,128)(2,1)}) %all-gather.8.cloned.1.call-update) | async-done | bytes 8388624 | tf_op jit(solution)/shard_map/all_gather | solution.py:66
  185.4 5.8 fusion.22
  193.4 191.2 %all-gather.4.cloned.1.call-done = bf16[4096,2048]{1,0:T(8,128)(2,1)} async-done(((bf16[64,2048]{1,0:T(8,128)(2,1)}), bf16[4096,2048]{1,0:T(8,128)(2,1)}) %all-gather.4.cloned.1.call-update) | async-done | bytes 16777232 | tf_op jit(solution)/shard_map/all_gather | solution.py:65
  384.6 20.9 %copy.28 = bf16[2048,4096]{1,0:T(8,128)(2,1)} copy(bf16[2048,4096]{0,1:T(8,128)(2,1)} %bitcast.119) | data formatting | bytes 33554432 | tf_op jit(solution)/shard_map/dot_general | solution.py:40
  405.5 8.3 fusion.20
  415.2 1.5 bitcast_reduce_fusion
  416.7 1.4 fusion.18
  418.2 0.9 fusion.17
  419.1 2.2 fusion.4
  421.3 1.6 fusion.35
  423.0 3.5 fusion.27
  426.5 4.0 fusion.24
  430.4 8.9 fusion.41
  439.4 1.6 copy.42
  440.9 1.6 copy.41
  442.5 1.5 pad_maximum_fusion
  444.1 72.9 %all-reduce.3.cloned.1.call-done = f32[512,1024]{1,0:T(8,128)} async-done(((f32[512,1024]{1,0:T(8,128)}), f32[512,1024]{1,0:T(8,128)}) %all-reduce.3.cloned.1.call-update) | async-done | bytes 2097168 | tf_op jit(solution)/shard_map/psum | solution.py:153
  517.0 1.4 copy.43
  518.4 1104.9 %all-reduce.5.cloned.1.call-done = f32[512,1024]{1,0:T(8,128)} async-done(((f32[512,1024]{1,0:T(8,128)}), f32[512,1024]{1,0:T(8,128)}) %all-reduce.5.cloned.1.call-update) | async-done | bytes 2097168 | tf_op jit(solution)/shard_map/psum | solution.py:153
  1623.3 2.4 divide_subtract_fusion
  (58 shorter events, 6.3 us)
Async XLA Ops:
  7.2 7.1 copy-start.1
  7.2 178.2 %copy-start.13 = (f32[4096]{0:T(1024)S(1)}, f32[4096]{0:T(1024)}, u32[]{:S(2)}) copy-start(f32[4096]{0:T(1024)} %param.10) | copy-start | bytes 49156
  7.2 28.8 %all-gather.6.cloned.1.call-start = ((), (), s32[]{:S(2)}) async-start(), calls=%async_computation.1 | async-start | bytes 1310720 | tf_op jit(solution)/shard_map/all_gather | solution.py:86
  9.3 176.1 %all-gather.8.cloned.1.call-start = ((), (), s32[]{:S(2)}) async-start(), calls=%async_computation.2 | async-start | bytes 8519680 | tf_op jit(solution)/shard_map/all_gather | solution.py:66
  10.0 374.6 %all-gather.4.cloned.1.call-start = ((), (), s32[]{:S(2)}) async-start(), calls=%async_computation | async-start | bytes 17039360 | tf_op jit(solution)/shard_map/all_gather | solution.py:65
  10.8 506.2 %all-reduce.3.cloned.1.call-start = ((), (), s32[]{:S(2)}) async-start(), calls=%async_computation.3 | async-start | bytes 4194304 | tf_op jit(solution)/shard_map/psum | solution.py:153
  11.8 3.0 copy-start.7
  384.6 20.9 %copy-start.2 = (bf16[1,256,4096]{2,1,0:T(8,128)(2,1)S(1)}, bf16[1,256,4096]{2,1,0:T(8,128)(2,1)}, u32[]{:S(2)}) copy-start(bf16[1,256,4096]{2,1,0:T(8,128)(2,1)} %param.9) | copy-start | bytes 6291460
  405.5 8.4 copy-start.8
  415.2 1.6 copy-start.6
  416.7 9.7 copy-start
  419.1 2.2 copy-start.12
  421.3 1.6 copy-start.4
  423.0 3.5 copy-start.11
  442.5 74.5 %copy-start.5 = (bf16[256,4,4,128]{0,3,2,1:T(8,128)(2,1)S(1)}, bf16[256,4,4,128]{0,3,2,1:T(8,128)(2,1)}, u32[]{:S(2)}) copy-start(bf16[256,4,4,128]{0,3,2,1:T(8,128)(2,1)} %get-tuple-element.30) | copy-start | bytes 3145732
  444.0 1179.3 %copy-start.3 = (f32[128,1024]{1,0:T(8,128)S(1)}, f32[128,1024]{1,0:T(8,128)}, u32[]{:S(2)}) copy-start(f32[128,1024]{1,0:T(8,128)} %param.15) | copy-start | bytes 1572868
  444.0 1179.3 %copy-start.9 = (f32[128,1024]{1,0:T(8,128)S(1)}, f32[128,1024]{1,0:T(8,128)}, u32[]{:S(2)}) copy-start(f32[128,1024]{1,0:T(8,128)} %param.16) | copy-start | bytes 1572868
  444.0 1179.3 %copy-start.10 = (f32[128,1024]{1,0:T(8,128)S(1)}, f32[128,1024]{1,0:T(8,128)}, u32[]{:S(2)}) copy-start(f32[128,1024]{1,0:T(8,128)} %param.17) | copy-start | bytes 1572868
  444.0 1179.3 %all-reduce.5.cloned.1.call-start = ((), (), s32[]{:S(2)}) async-start(), calls=%async_computation.4 | async-start | bytes 4194304 | tf_op jit(solution)/shard_map/psum | solution.py:153
Sparse Core Ops, SparseCore 0:
  10.4 25.5 all-gather.5
  39.6 145.6 all-gather.7
  189.0 195.5 all-gather.3
  444.2 72.7 all-reduce.2
  519.4 1103.8 all-reduce.4
